TPU v7x, 32 devices: a whole 2x2x4 slice. The times are simulated.
32 devices in a mesh: pix: 8 (over z, y), rep: 4 (over x, core).
Axes of the slice: x: 2, y: 2, z: 4, core: 2. Of those that a mesh axis runs over, the one named last changes fastest.
Arguments:
- sky_cube: float32 [4, 512, 65536], P('rep', None, 'pix'), may hold values from -6 to 10
- pixel_mask: int32 [4, 65536], P('rep', 'pix'), may hold values 0 or 1
- noise_cov: float32 [512, 512], replicated, may hold values from -1 to 2, as said below
Outputs:
- power_cube: float32 [4, 512, 65536], P('rep', 'pix')
Inputs may be any that keep to these rules, and one draw needn't show every extreme that they name: `noise_cov`: symmetric; each diagonal entry exceeds the sum of magnitudes off the diagonal in its row.
All inputs are finite; a program needn't handle non-finite values. No bound on the sum of `pixel_mask` on one device may be relied on, other than what follows from the above.
Results may differ from a plain program's by a relative error of at most 0.00012.
Values sent between devices are 32-bit elements; how exact they have to be, the bound alone decides.
A program may use at most 320 MiB of HBM per device.

v0:
```python
import math
import jax
import jax.numpy as jnp
from jax import lax
from jax.sharding import PartitionSpec as P

F = 512
SY = 256
SX = 256
HI = lax.Precision.HIGHEST


def dft_pair(length):
    idx = jnp.arange(length, dtype=jnp.int32)
    phase = (idx[:, None] * idx[None, :] % length).astype(jnp.float32) * (2.0 * math.pi / length)
    return (jnp.cos(phase), jnp.sin(phase))


def los_table(length):
    idx = jnp.arange(length, dtype=jnp.int32)
    half_len = length // 2
    freq = jnp.where(idx <= half_len, idx, idx - half_len)
    phase = (freq[:, None] * idx[None, :] % length).astype(jnp.float32) * (2.0 * math.pi / length)
    values = jnp.where((idx <= half_len)[:, None], jnp.cos(phase), jnp.sin(phase))
    edge = jnp.logical_or(idx == 0, idx == half_len)
    scale = jnp.where(edge, math.sqrt(1.0 / length), math.sqrt(2.0 / length)).astype(jnp.float32)
    return values * scale[:, None]


def sky_power(planes, rows_y, cols_x):
    count = planes.shape[0]
    field = planes.reshape(count, rows_y, cols_x)
    cos_x, sin_x = dft_pair(cols_x)
    cos_y, sin_y = dft_pair(rows_y)
    both_x = jnp.concatenate([cos_x, sin_x], axis=1)
    both_y = jnp.concatenate([cos_y, sin_y], axis=0)
    first = jnp.einsum("kyx,xw->kyw", field, both_x, precision=HI)
    second = jnp.einsum("vy,kyw->kvw", both_y, first, precision=HI)
    real_part = second[:, :rows_y, :cols_x] - second[:, rows_y:, cols_x:]
    imag_part = -(second[:, rows_y:, :cols_x] + second[:, :rows_y, cols_x:])
    power_map = (real_part * real_part + imag_part * imag_part) / float(rows_y * cols_x)
    return power_map.reshape(count, rows_y * cols_x)


def reduce_cov(partial_value):
    summed = lax.psum(partial_value, ("pix", "rep"))
    return summed


def plane_power(planes):
    return sky_power(planes[0], SY, SX)[None]


def local(sky_cube, pixel_mask, noise_cov):
    live = pixel_mask[0].astype(jnp.float32)
    masked = sky_cube[0] * live[None, :]
    table = los_table(F)
    partial_value = jnp.dot(masked, masked.T, precision=HI)
    data_cov = reduce_cov(partial_value)
    scale_all = float(lax.axis_size("pix") * lax.axis_size("rep") * masked.shape[1])
    regular = data_cov / scale_all + noise_cov
    factor = jnp.linalg.cholesky(regular)
    filter_t = jax.scipy.linalg.cho_solve((factor, True), noise_cov)
    folded_map = jnp.dot(table, filter_t.T, precision=HI)
    spectra = jnp.dot(folded_map, masked, precision=HI)
    owners = lax.axis_size("pix")
    stacked = spectra.reshape(owners, spectra.shape[0] // owners, spectra.shape[1])
    return plane_power(lax.all_to_all(stacked, "pix", split_axis=0, concat_axis=2, tiled=True))


def solution(mesh):
    placed = (P("rep", None, "pix"), P("rep", "pix"), P())
    return jax.shard_map(
        local, mesh=mesh, in_specs=placed, out_specs=P("rep", "pix", None), check_vma=False
    )
```

profile of v0, /device:TPU:0, one launch (start us, length us, event | category | flops | bytes accessed | tf_op | source)
XLA Modules:
  0.0 922.2 jit_solution(2023043148262930889)
XLA Ops:
  7.3 32.8 %fusion.6 = f32[512,512]{0,1:T(8,128)} fusion(f32[1,512,8192]{2,1,0:T(8,128)} %param.3, f32[8192]{0:T(1024)S(1)} %bitcast.88), kind=kOutput, calls=%fused_computation.11 | convolution fusion | flops 25773998080 | bytes 17858560 | tf_op jit(solution)/shard_map/dot_general | solution.py:58
  40.5 133.3 %all-reduce.3.cloned.1.call-done = f32[512,512]{0,1:T(8,128)} async-done(((f32[512,512]{0,1:T(8,128)}), f32[512,512]{0,1:T(8,128)}) %all-reduce.3.cloned.1.call-update) | async-done | bytes 1048592 | tf_op jit(solution)/shard_map/psum | solution.py:46
  173.8 1.4 multiply_add_fusion
  176.8 11.7 %cholesky.104 = f32[128,128]{1,0:T(8,128)S(1)} custom-call(f32[128,128]{1,0:T(8,128)S(1)} %cholesky.266), custom_call_target="Cholesky" | custom-call | tf_op jit(solution)/shard_map/jit(cholesky)/cholesky | solution.py:62
  188.5 9.8 %custom-call.34 = f32[1,128,128]{1,2,0:T(8,128)S(1)} custom-call(f32[1,128,128]{2,1,0:T(8,128)S(1)} %get-tuple-element.32), custom_call_target="InvertDiagBlocksLowerTriangular" | custom-call | tf_op jit(solution)/shard_map/jit(cholesky)/cholesky | solution.py:62
  198.5 1.2 constant_dynamic-update-slice_fusion.2
  199.7 1.3 convolution_subtract_fusion.6
  201.0 11.7 %cholesky.217 = f32[128,128]{1,0:T(8,128)S(1)} custom-call(f32[128,128]{1,0:T(8,128)S(1)} %cholesky.270), custom_call_target="Cholesky" | custom-call | tf_op jit(solution)/shard_map/jit(cholesky)/cholesky | solution.py:62
  212.8 10.0 %custom-call.35 = f32[1,128,128]{1,2,0:T(8,128)S(1)} custom-call(f32[1,128,128]{2,1,0:T(8,128)S(1)} %get-tuple-element.29), custom_call_target="InvertDiagBlocksLowerTriangular" | custom-call | tf_op jit(solution)/shard_map/jit(cholesky)/cholesky | solution.py:62
  223.0 1.3 convolution_subtract_fusion.7
  224.3 11.7 %cholesky.238 = f32[128,128]{1,0:T(8,128)S(1)} custom-call(f32[128,128]{1,0:T(8,128)S(1)} %cholesky.275), custom_call_target="Cholesky" | custom-call | tf_op jit(solution)/shard_map/jit(cholesky)/cholesky | solution.py:62
  236.8 9.8 %custom-call.36 = f32[1,128,128]{1,2,0:T(8,128)S(1)} custom-call(f32[1,128,128]{2,1,0:T(8,128)S(1)} %get-tuple-element.26), custom_call_target="InvertDiagBlocksLowerTriangular" | custom-call | tf_op jit(solution)/shard_map/jit(cholesky)/cholesky | solution.py:62
  246.8 1.2 convolution_subtract_fusion.8
  248.0 12.1 %cholesky.255 = f32[128,128]{1,0:T(8,128)S(1)} custom-call(f32[128,128]{1,0:T(8,128)S(1)} %convolution_subtract_fusion.8), custom_call_target="Cholesky" | custom-call | tf_op jit(solution)/shard_map/jit(cholesky)/cholesky | solution.py:62
  264.1 8.5 while.1
  264.8 1.4 bitcast_dynamic-update-slice_fusion.2
  266.9 1.4 bitcast_dynamic-update-slice_fusion.2
  269.1 1.4 bitcast_dynamic-update-slice_fusion.2
  271.2 1.4 bitcast_dynamic-update-slice_fusion.2
  272.6 39.3 %custom-call.37 = f32[4,128,128]{1,2,0:T(8,128)S(1)} custom-call(f32[4,128,128]{2,1,0:T(8,128)S(1)} %get-tuple-element.12), custom_call_target="InvertDiagBlocksLowerTriangular" | custom-call | tf_op jit(solution)/shard_map/jit(_cho_solve)/triangular_solve | solution.py:63
  318.2 6.1 fusion.15
  324.3 31.8 %fusion.4 = f32[8,64,8192]{2,1,0:T(8,128)} fusion(f32[8,64,512]{2,1,0:T(8,128)S(1)} %bitcast.87, f32[1,512,8192]{2,1,0:T(8,128)} %param.3, f32[8192]{0:T(1024)S(1)} %bitcast.89), kind=kOutput, calls=%fused_computation.9 | convolution fusion | flops 25773998080 | bytes 34635776 | tf_op jit(solution)/shard_map/dot_general | solution.py:65
  356.1 5.8 all-to-all-start
  361.9 1.0 fusion.80
  363.0 361.2 %all-to-all-done = f32[8,64,8192]{2,1,0:T(8,128)} async-done(((f32[8,64,8192]{2,1,0:T(8,128)}), f32[8,64,8192]{2,1,0:T(8,128)}, u32[]{:S(2)}, u32[]{:S(2)}) %all-to-all-start) | async-done | bytes 16777248 | tf_op jit(solution)/shard_map/all_to_all | solution.py:68
  724.1 17.8 %copy.10 = f32[1,64,8,8192]{3,2,1,0:T(8,128)} copy(f32[1,64,8,8192]{3,1,2,0:T(8,128)} %bitcast.16) | data formatting | bytes 33554432 | tf_op jit(solution)/shard_map/all_to_all | solution.py:68
  741.9 18.0 %reshape_squeeze.3 = f32[64,256,256]{2,1,0:T(8,128)} reshape(f32[1,64,8,8192]{3,2,1,0:T(8,128)} %copy.10) | data formatting | bytes 33554432 | tf_op jit(solution)/shard_map/reshape;squeeze | solution.py:32
  759.9 33.4 %fusion.50 = f32[64,256,512]{1,2,0:T(8,128)} fusion(f32[64,256,256]{2,1,0:T(8,128)} %reshape_squeeze.3, f32[256,256]{1,0:T(8,128)S(1)} %get-tuple-element.37, f32[256,256]{1,0:T(8,128)S(1)} %get-tuple-element.38), kind=kOutput, calls=%fused_computation.71 | convolution fusion | flops 25769934848 | bytes 50855936 | tf_op jit(solution)/shard_map/kyx,xw->kyw/dot_general | solution.py:37
  793.3 61.2 %convolution_bitcast_fusion = f32[64,512,512]{1,2,0:T(8,128)} fusion(f32[64,256,512]{1,2,0:T(8,128)} %fusion.50, f32[512,256,1]{1,0,2:T(8,128)S(1)} %maximum_bitcast_fusion.6), kind=kOutput, calls=%fused_computation.2 | convolution fusion | flops 51539607552 | bytes 101187584 | tf_op jit(solution)/shard_map/vy,kyw->kvw/dot_general | solution.py:38
  854.5 28.6 %fusion.2 = f32[64,256,256]{1,2,0:T(8,128)} fusion(f32[64,512,512]{1,2,0:T(8,128)} %convolution_bitcast_fusion), kind=kLoop, calls=%fused_computation.6 | loop fusion | flops 25165824 | bytes 83886080 | tf_op jit(solution)/shard_map/div | solution.py:41
  883.1 17.5 %copy.11 = f32[64,256,256]{2,1,0:T(8,128)} copy(f32[64,256,256]{1,2,0:T(8,128)} %fusion.2) | data formatting | bytes 33554432 | tf_op jit(solution)/shard_map/div | solution.py:41
  900.5 14.6 %broadcast_in_dim_reshape.3 = f32[1,64,65536]{2,1,0:T(8,128)} reshape(f32[64,256,256]{2,1,0:T(8,128)} %copy.11) | data formatting | bytes 33554432 | tf_op jit(solution)/shard_map/broadcast_in_dim;reshape | solution.py:51
  (53 shorter events, 14.4 us)
Async XLA Ops:
  6.5 167.3 %all-reduce.3.cloned.1.call-start = ((), (), s32[]{:S(2)}) async-start(), calls=%async_computation.1 | async-start | bytes 2097152 | tf_op jit(solution)/shard_map/psum | solution.py:46
  7.3 32.8 %copy-start = (f32[512,512]{1,0:T(8,128)S(1)}, f32[512,512]{1,0:T(8,128)}, u32[]{:S(2)}) copy-start(f32[512,512]{1,0:T(8,128)} %param.5) | copy-start | bytes 3145732
  175.8 1.0 copy-start.1
  356.1 368.0 %all-to-all-start = ((f32[8,64,8192]{2,1,0:T(8,128)}), f32[8,64,8192]{2,1,0:T(8,128)}, u32[]{:S(2)}, u32[]{:S(2)}) async-start(f32[8,64,8192]{2,1,0:T(8,128)} %fusion.4), calls=%async_computation | async-start | bytes 33554432 | tf_op jit(solution)/shard_map/all_to_all | solution.py:68
Sparse Core Ops, SparseCore 0:
  40.2 133.4 all-reduce.2
where the time goes:
time: 929 us; the launch traced here: 922 us
  waiting for transfers between devices  494 us (53%)
  matrix products  177 us (19%)
  other arithmetic  151 us (16%)
  local copies, waits for them, and re-layouts  78 us (8%)
  between operations  16.6 us (2%)
    all_to_all x1, waiting for transfers between devices, local(): lax.all_to_all(stacked, 'pix', split_axis=0, concat_axis=2, tiled=True)  361 us
    psum x1, waiting for transfers between devices, reduce_cov(): summed = lax.psum(partial_value, ('pix', 'rep'))  133 us
    another operation x14, other arithmetic, local(): factor = jnp.linalg.cholesky(regular)  79 us
    dot_general x1, matrix products, sky_power(): second = jnp.einsum('vy,kyw->kvw', both_y, first, precision=HI)  61.2 us
    another operation x3, other arithmetic, local(): filter_t = jax.scipy.linalg.cho_solve((factor, True), noise_cov)  39.4 us
    dot_general x1, matrix products, sky_power(): first = jnp.einsum('kyx,xw->kyw', field, both_x, precision=HI)  33.4 us
    dot_general x1, matrix products, local(): partial_value = jnp.dot(masked, masked.T, precision=HI)  32.8 us
    dot_general x1, matrix products, local(): spectra = jnp.dot(folded_map, masked, precision=HI)  31.8 us
  transfers between devices with their start and end apart: 2, of which 2 were waited for; matrix products, arithmetic and copies ran while one was open for 0% of the time, Pallas kernels for 0%

commit v1 on v0

--- a/solution.py
+++ b/solution.py
@@ -43,7 +43,7 @@
 
 
 def reduce_cov(partial_value):
-    summed = lax.psum(partial_value, ("pix", "rep"))
+    summed = lax.psum(lax.psum(partial_value, "rep"), "pix")
     return summed
 
 

time: 929 us -> 917 us (0.987)
  waiting for transfers between devices: 494 us -> 483 us
    psum x1 -> x2, waiting for transfers between devices: 133 us -> 121 us  [reduce_cov(): summed = lax.psum(lax.psum(partial_value, 'rep'), 'pix')]
  transfers between devices with their start and end apart: 2 -> 3, of which waited for: 2 -> 3; matrix products, arithmetic and copies ran while one was open for 0% -> 0% of each run, Pallas kernels for 0% -> 0%
where the time goes in v1:
time: 917 us; the launch traced here: 910 us
  waiting for transfers between devices  483 us (53%)
  matrix products  176 us (19%)
  other arithmetic  151 us (16%)
  local copies, waits for them, and re-layouts  78 us (9%)
  between operations  16.6 us (2%)
    all_to_all x1, waiting for transfers between devices, local(): lax.all_to_all(stacked, 'pix', split_axis=0, concat_axis=2, tiled=True)  362 us
    psum x2, waiting for transfers between devices, reduce_cov(): summed = lax.psum(lax.psum(partial_value, 'rep'), 'pix')  121 us
    another operation x14, other arithmetic, local(): factor = jnp.linalg.cholesky(regular)  79 us
    dot_general x1, matrix products, sky_power(): second = jnp.einsum('vy,kyw->kvw', both_y, first, precision=HI)  61.2 us
    another operation x3, other arithmetic, local(): filter_t = jax.scipy.linalg.cho_solve((factor, True), noise_cov)  39.4 us
    dot_general x1, matrix products, sky_power(): first = jnp.einsum('kyx,xw->kyw', field, both_x, precision=HI)  33.4 us
    dot_general x1, matrix products, local(): partial_value = jnp.dot(masked, masked.T, precision=HI)  32.3 us
    dot_general x1, matrix products, local(): spectra = jnp.dot(folded_map, masked, precision=HI)  31.8 us
  transfers between devices with their start and end apart: 3, of which 3 were waited for; matrix products, arithmetic and copies ran while one was open for 0% of the time, Pallas kernels for 0%

profile of v1, /device:TPU:0, one launch (start us, length us, event | category | flops | bytes accessed | tf_op | source)
XLA Modules:
  0.0 910.4 jit_solution(17190444218025766808)
XLA Ops:
  7.3 32.3 %fusion.6 = f32[512,512]{0,1:T(8,128)} fusion(f32[1,512,8192]{2,1,0:T(8,128)} %param.3, f32[8192]{0:T(1024)S(1)} %bitcast.88), kind=kOutput, calls=%fused_computation.11 | convolution fusion | flops 25773998080 | bytes 17858560 | tf_op jit(solution)/shard_map/dot_general | solution.py:58
  40.2 38.7 %all-reduce.4.cloned.1.call-done = f32[512,512]{0,1:T(8,128)} async-done(((f32[512,512]{0,1:T(8,128)}), f32[512,512]{0,1:T(8,128)}) %all-reduce.4.cloned.1.call-update) | async-done | bytes 1048592 | tf_op jit(solution)/shard_map/psum | solution.py:46
  79.3 81.9 %all-reduce.6.cloned.1.call-done = f32[512,512]{0,1:T(8,128)} async-done(((f32[512,512]{0,1:T(8,128)}), f32[512,512]{0,1:T(8,128)}) %all-reduce.6.cloned.1.call-update) | async-done | bytes 1048592 | tf_op jit(solution)/shard_map/psum | solution.py:46
  161.2 1.4 multiply_add_fusion
  164.2 11.7 %cholesky.104 = f32[128,128]{1,0:T(8,128)S(1)} custom-call(f32[128,128]{1,0:T(8,128)S(1)} %cholesky.266), custom_call_target="Cholesky" | custom-call | tf_op jit(solution)/shard_map/jit(cholesky)/cholesky | solution.py:62
  175.9 9.8 %custom-call.34 = f32[1,128,128]{1,2,0:T(8,128)S(1)} custom-call(f32[1,128,128]{2,1,0:T(8,128)S(1)} %get-tuple-element.32), custom_call_target="InvertDiagBlocksLowerTriangular" | custom-call | tf_op jit(solution)/shard_map/jit(cholesky)/cholesky | solution.py:62
  185.9 1.2 constant_dynamic-update-slice_fusion.2
  187.1 1.3 convolution_subtract_fusion.6
  188.4 11.7 %cholesky.217 = f32[128,128]{1,0:T(8,128)S(1)} custom-call(f32[128,128]{1,0:T(8,128)S(1)} %cholesky.270), custom_call_target="Cholesky" | custom-call | tf_op jit(solution)/shard_map/jit(cholesky)/cholesky | solution.py:62
  200.2 10.0 %custom-call.35 = f32[1,128,128]{1,2,0:T(8,128)S(1)} custom-call(f32[1,128,128]{2,1,0:T(8,128)S(1)} %get-tuple-element.29), custom_call_target="InvertDiagBlocksLowerTriangular" | custom-call | tf_op jit(solution)/shard_map/jit(cholesky)/cholesky | solution.py:62
  210.4 1.3 convolution_subtract_fusion.7
  211.7 11.7 %cholesky.238 = f32[128,128]{1,0:T(8,128)S(1)} custom-call(f32[128,128]{1,0:T(8,128)S(1)} %cholesky.275), custom_call_target="Cholesky" | custom-call | tf_op jit(solution)/shard_map/jit(cholesky)/cholesky | solution.py:62
  224.2 9.8 %custom-call.36 = f32[1,128,128]{1,2,0:T(8,128)S(1)} custom-call(f32[1,128,128]{2,1,0:T(8,128)S(1)} %get-tuple-element.26), custom_call_target="InvertDiagBlocksLowerTriangular" | custom-call | tf_op jit(solution)/shard_map/jit(cholesky)/cholesky | solution.py:62
  234.2 1.2 convolution_subtract_fusion.8
  235.4 12.1 %cholesky.255 = f32[128,128]{1,0:T(8,128)S(1)} custom-call(f32[128,128]{1,0:T(8,128)S(1)} %convolution_subtract_fusion.8), custom_call_target="Cholesky" | custom-call | tf_op jit(solution)/shard_map/jit(cholesky)/cholesky | solution.py:62
  251.5 8.5 while.1
  252.2 1.4 bitcast_dynamic-update-slice_fusion.2
  254.3 1.4 bitcast_dynamic-update-slice_fusion.2
  256.5 1.4 bitcast_dynamic-update-slice_fusion.2
  258.6 1.4 bitcast_dynamic-update-slice_fusion.2
  260.0 39.3 %custom-call.37 = f32[4,128,128]{1,2,0:T(8,128)S(1)} custom-call(f32[4,128,128]{2,1,0:T(8,128)S(1)} %get-tuple-element.12), custom_call_target="InvertDiagBlocksLowerTriangular" | custom-call | tf_op jit(solution)/shard_map/jit(_cho_solve)/triangular_solve | solution.py:63
  305.6 6.1 fusion.15
  311.7 31.8 %fusion.4 = f32[8,64,8192]{2,1,0:T(8,128)} fusion(f32[8,64,512]{2,1,0:T(8,128)S(1)} %bitcast.87, f32[1,512,8192]{2,1,0:T(8,128)} %param.3, f32[8192]{0:T(1024)S(1)} %bitcast.89), kind=kOutput, calls=%fused_computation.9 | convolution fusion | flops 25773998080 | bytes 34635776 | tf_op jit(solution)/shard_map/dot_general | solution.py:65
  343.5 5.8 all-to-all-start
  350.3 362.0 %all-to-all-done = f32[8,64,8192]{2,1,0:T(8,128)} async-done(((f32[8,64,8192]{2,1,0:T(8,128)}), f32[8,64,8192]{2,1,0:T(8,128)}, u32[]{:S(2)}, u32[]{:S(2)}) %all-to-all-start) | async-done | bytes 16777248 | tf_op jit(solution)/shard_map/all_to_all | solution.py:68
  712.3 17.8 %copy.10 = f32[1,64,8,8192]{3,2,1,0:T(8,128)} copy(f32[1,64,8,8192]{3,1,2,0:T(8,128)} %bitcast.16) | data formatting | bytes 33554432 | tf_op jit(solution)/shard_map/all_to_all | solution.py:68
  730.1 18.0 %reshape_squeeze.3 = f32[64,256,256]{2,1,0:T(8,128)} reshape(f32[1,64,8,8192]{3,2,1,0:T(8,128)} %copy.10) | data formatting | bytes 33554432 | tf_op jit(solution)/shard_map/reshape;squeeze | solution.py:32
  748.1 33.4 %fusion.50 = f32[64,256,512]{1,2,0:T(8,128)} fusion(f32[64,256,256]{2,1,0:T(8,128)} %reshape_squeeze.3, f32[256,256]{1,0:T(8,128)S(1)} %get-tuple-element.37, f32[256,256]{1,0:T(8,128)S(1)} %get-tuple-element.38), kind=kOutput, calls=%fused_computation.71 | convolution fusion | flops 25769934848 | bytes 50855936 | tf_op jit(solution)/shard_map/kyx,xw->kyw/dot_general | solution.py:37
  781.5 61.2 %convolution_bitcast_fusion = f32[64,512,512]{1,2,0:T(8,128)} fusion(f32[64,256,512]{1,2,0:T(8,128)} %fusion.50, f32[512,256,1]{1,0,2:T(8,128)S(1)} %maximum_bitcast_fusion.6), kind=kOutput, calls=%fused_computation.2 | convolution fusion | flops 51539607552 | bytes 101187584 | tf_op jit(solution)/shard_map/vy,kyw->kvw/dot_general | solution.py:38
  842.7 28.6 %fusion.2 = f32[64,256,256]{1,2,0:T(8,128)} fusion(f32[64,512,512]{1,2,0:T(8,128)} %convolution_bitcast_fusion), kind=kLoop, calls=%fused_computation.6 | loop fusion | flops 25165824 | bytes 83886080 | tf_op jit(solution)/shard_map/div | solution.py:41
  871.3 17.5 %copy.11 = f32[64,256,256]{2,1,0:T(8,128)} copy(f32[64,256,256]{1,2,0:T(8,128)} %fusion.2) | data formatting | bytes 33554432 | tf_op jit(solution)/shard_map/div | solution.py:41
  888.7 14.6 %broadcast_in_dim_reshape.3 = f32[1,64,65536]{2,1,0:T(8,128)} reshape(f32[64,256,256]{2,1,0:T(8,128)} %copy.11) | data formatting | bytes 33554432 | tf_op jit(solution)/shard_map/broadcast_in_dim;reshape | solution.py:51
  (56 shorter events, 16.0 us)
Async XLA Ops:
  6.5 72.3 %all-reduce.4.cloned.1.call-start = ((), (), s32[]{:S(2)}) async-start(), calls=%async_computation.1 | async-start | bytes 2097152 | tf_op jit(solution)/shard_map/psum | solution.py:46
  7.3 71.6 %copy-start = (f32[512,512]{1,0:T(8,128)S(1)}, f32[512,512]{1,0:T(8,128)}, u32[]{:S(2)}) copy-start(f32[512,512]{1,0:T(8,128)} %param.5) | copy-start | bytes 3145732
  39.7 121.5 %all-reduce.6.cloned.1.call-start = ((), (), s32[]{:S(2)}) async-start(), calls=%async_computation.2 | async-start | bytes 2097152 | tf_op jit(solution)/shard_map/psum | solution.py:46
  163.2 1.0 copy-start.1
  343.5 368.8 %all-to-all-start = ((f32[8,64,8192]{2,1,0:T(8,128)}), f32[8,64,8192]{2,1,0:T(8,128)}, u32[]{:S(2)}, u32[]{:S(2)}) async-start(f32[8,64,8192]{2,1,0:T(8,128)} %fusion.4), calls=%async_computation | async-start | bytes 33554432 | tf_op jit(solution)/shard_map/all_to_all | solution.py:68
Sparse Core Ops, SparseCore 0:
  39.8 39.0 all-reduce.3
  82.4 78.7 all-reduce.5
